TPU v7x, 32 devices: a whole 2x2x4 slice. The times are simulated.
32 devices in a mesh: dp: 8 (over z, y), fsdp: 4 (over x, core).
Axes of the slice: x: 2, y: 2, z: 4, core: 2. Of those that a mesh axis runs over, the one named last changes fastest.
Arguments:
- tiles: bfloat16 [768, 4096], P('fsdp', 'dp'), may hold values from -6 to 6
- kernel: bfloat16 [49, 768], P(None, 'fsdp'), may hold values from -0.875 to 0.875
- norm_gain: bfloat16 [768], P('fsdp'), may hold values from 0.099609375 to 1.8984375
- w_up: bfloat16 [768, 1536], P('dp', 'fsdp'), may hold values from -0.21875 to 0.21875
- w_down: bfloat16 [768, 1536], P('dp', 'fsdp'), may hold values from -0.15625 to 0.15625
- layer_scale: bfloat16 [768], P('fsdp'), may hold values from 0.5 to 2
- neighbors: int32 [64, 4, 2], P('dp'), may hold values from -1 to 63, as said below
- shifts: int32 [64, 4, 2], P('dp'), may hold values from -8 to 7, as said below
- halo_widths: int32 [64, 4], P('dp'), may hold values from 1 to 3
- land: int32 [64, 8, 8], P('dp'), may hold values 0 or 1
- cotangent: bfloat16 [768, 4096], P('fsdp', 'dp'), may hold values from -6 to 6
Outputs:
- block_out: bfloat16 [768, 4096], P('fsdp', 'dp')
- tile_grad: bfloat16 [768, 4096], P('fsdp', 'dp')
- up_grad: float32 [768, 1536], P('dp', 'fsdp')
- down_grad: float32 [768, 1536], P('dp', 'fsdp')
Inputs may be any that keep to these rules, and one draw needn't show every extreme that they name: `neighbors`: faces are north, south, west, east. Tile t is held by index t // 8 of dp. A named north or south neighbour is held by the same index of dp as the tile, a west one by the index before, an east one by the index after. Adjacency is symmetric: a cell taken from a neighbour's edge belongs to the tile that takes the facing cell of it. Entry 0 of a face holds shifts 0 to 7, entry 1 shifts -8 to -1; an entry that names no tile has shift 0, and north and south shifts are 0.
All inputs are finite; a program needn't handle non-finite values. No bound on the sum of `land` on one device may be relied on, other than what follows from the above.
Results may differ from a plain program's by a relative error of at most 0.0095.
Values may be sent and summed in bfloat16 or wider, within the bound.
No kernel may reach another device: no remote copies, remote signals or barrier semaphores. Data moves between devices by JAX's collectives and lax.ppermute only.
A program may use at most 64 MiB of HBM per device.

v0:
```python
import math

import jax
import jax.numpy as jnp
from jax import lax
from jax.sharding import PartitionSpec as P

root_half = 1.0 / math.sqrt(2.0)
root_tau = 1.0 / math.sqrt(2.0 * math.pi)


def padded_2(block, sides, width):
    for axis, dim in sides:
        count = lax.axis_size(axis)
        forward = [(i, i + 1) for i in range(count - 1)]
        backward = [(target, source) for source, target in forward]
        low = lax.ppermute(
            lax.slice_in_dim(block, block.shape[dim] - width, None, axis=dim), axis, forward
        )
        high = lax.ppermute(lax.slice_in_dim(block, 0, width, axis=dim), axis, backward)
        block = jnp.concatenate([low, block, high], axis=dim)
    return block


def gelu_value(hidden):
    return 0.5 * hidden * (1.0 + jax.scipy.special.erf(hidden * root_half))


def gelu_slope(hidden):
    return (
        0.5 * (1.0 + jax.scipy.special.erf(hidden * root_half))
        + hidden * jnp.exp(-0.5 * hidden * hidden) * root_tau
    )


def depth_keep(widths_face, far_first):
    layer_index = jnp.arange(3, dtype=jnp.int32)
    if far_first:
        depth_value = 3 - layer_index
    else:
        depth_value = layer_index + 1
    return depth_value[None, :] <= widths_face[:, None]


def depthwise_flat(padded, kernel):
    channels, tile_count, wide, _ = padded.shape
    total = tile_count * wide * wide
    flat = jnp.pad(padded.reshape(channels, total), ((0, 0), (0, 6 * wide + 6)))
    taps = kernel.astype(jnp.float32)
    summed = jnp.zeros((channels, total), jnp.float32)
    for row_tap in range(7):
        for col_tap in range(7):
            offset = row_tap * wide + col_tap
            summed = (
                summed
                + flat[:, offset : offset + total].astype(jnp.float32)
                * taps[row_tap * 7 + col_tap][:, None]
            )
    side_len = wide - 6
    return summed.reshape(channels, tile_count, wide, wide)[:, :, :side_len, :side_len]


def depthwise_back_flat(grad_grid, kernel):
    channels, tile_count, side_len, _ = grad_grid.shape
    wide = side_len + 6
    total = tile_count * wide * wide
    lead = 6 * wide + 6
    placed = jnp.pad(grad_grid.astype(jnp.float32), ((0, 0), (0, 0), (0, 6), (0, 6))).reshape(
        channels, total
    )
    placed = jnp.pad(placed, ((0, 0), (lead, 0)))
    taps = kernel.astype(jnp.float32)
    summed = jnp.zeros((channels, total), jnp.float32)
    for row_tap in range(7):
        for col_tap in range(7):
            offset = row_tap * wide + col_tap
            summed = (
                summed
                + placed[:, lead - offset : lead - offset + total]
                * taps[row_tap * 7 + col_tap][:, None]
            )
    return summed.reshape(channels, tile_count, wide, wide)


def selection(neighbor_ids, shift_values, tile_count, side_len):
    position = jnp.arange(side_len, dtype=jnp.int32)
    source_tile = jnp.arange(tile_count, dtype=jnp.int32)
    summed = jnp.zeros((tile_count, side_len, tile_count, side_len), jnp.float32)
    for which_entry in range(2):
        owner_tile = neighbor_ids[:, which_entry]
        slot_index = jnp.where(owner_tile >= 0, owner_tile % tile_count, -1)
        along_edge = position[None, :] + shift_values[:, which_entry][:, None]
        tile_hit = slot_index[:, None] == source_tile[None, :]
        row_hit = along_edge[:, :, None] == position[None, None, :]
        summed = summed + (tile_hit[:, None, :, None] & row_hit[:, :, None, :]).astype(jnp.float32)
    return summed.reshape(tile_count * side_len, tile_count * side_len)


def per_device(
    tiles,
    kernel,
    norm_gain,
    w_up,
    w_down,
    layer_scale,
    neighbors,
    shifts,
    halo_widths,
    land,
    cotangent,
):
    channels = tiles.shape[0]
    tile_count, side_len = (land.shape[0], land.shape[1])
    row_count = tile_count * side_len * side_len
    face_cols = tile_count * side_len
    full_width = channels * lax.axis_size("fsdp")
    grid_in = tiles.reshape(channels, tile_count, side_len, side_len)
    north_src = jnp.transpose(grid_in[:, :, side_len - 3 :, :], (2, 0, 1, 3))
    south_src = jnp.transpose(grid_in[:, :, :3, :], (2, 0, 1, 3))
    west_src = jnp.transpose(grid_in[:, :, :, side_len - 3 :], (3, 0, 1, 2))
    east_src = jnp.transpose(grid_in[:, :, :, :3], (3, 0, 1, 2))
    edges = padded_2(jnp.stack([east_src, west_src]), (("dp", 0),), 1)
    faces = (north_src, south_src, edges[0], edges[3])
    selectors = []
    masks = []
    halos = []
    for face_index in range(4):
        selector = selection(neighbors[:, face_index], shifts[:, face_index], tile_count, side_len)
        keep = depth_keep(halo_widths[:, face_index], face_index in (0, 2))
        keep_mask = jnp.transpose(keep)[:, None, :, None]
        picked = jnp.dot(
            faces[face_index].reshape(3 * channels, face_cols),
            selector.T.astype(jnp.bfloat16),
            preferred_element_type=jnp.float32,
        )
        halos.append(
            jnp.where(keep_mask, picked.reshape(3, channels, tile_count, side_len), 0.0).astype(
                jnp.bfloat16
            )
        )
        selectors.append(selector)
        masks.append(keep_mask)
    up_full, down_full = (
        lax.all_gather(w_up, "dp", axis=0, tiled=True),
        lax.all_gather(w_down, "dp", axis=0, tiled=True),
    )
    corner = jnp.zeros((channels, tile_count, 3, 3), jnp.bfloat16)
    upper = jnp.concatenate([corner, jnp.transpose(halos[0], (1, 2, 0, 3)), corner], axis=3)
    lower = jnp.concatenate([corner, jnp.transpose(halos[1], (1, 2, 0, 3)), corner], axis=3)
    middle = jnp.concatenate(
        [jnp.transpose(halos[2], (1, 2, 3, 0)), grid_in, jnp.transpose(halos[3], (1, 2, 3, 0))],
        axis=3,
    )
    padded = jnp.concatenate([upper, middle, lower], axis=2)
    conv = depthwise_flat(padded, kernel)
    conv_rows = conv.reshape(channels, row_count).astype(jnp.bfloat16)
    gain_f = norm_gain.astype(jnp.float32)[:, None]
    values = lax.optimization_barrier(conv_rows).astype(jnp.float32)
    row_total, row_squares = lax.psum(
        (jnp.sum(values, axis=0), jnp.sum(values * values, axis=0)), "fsdp"
    )
    row_mean = row_total / full_width
    inv_scale = lax.rsqrt(row_squares / full_width - row_mean * row_mean + 1e-06)
    centered = (values - row_mean[None, :]) * inv_scale[None, :]
    normed = lax.all_gather((centered * gain_f).astype(jnp.bfloat16), "fsdp", axis=0, tiled=True)
    pre_act = lax.dot_general(
        normed, up_full, (((0,), (0,)), ((), ())), preferred_element_type=jnp.float32
    )
    hidden = gelu_value(pre_act).astype(jnp.bfloat16)
    partial_out = lax.dot_general(
        down_full, hidden, (((1,), (1,)), ((), ())), preferred_element_type=jnp.float32
    )
    mixed = lax.psum_scatter(
        partial_out.astype(jnp.bfloat16), "fsdp", scatter_dimension=0, tiled=True
    ).astype(jnp.float32)
    scale_f = layer_scale.astype(jnp.float32)[:, None]
    block_out = (tiles.astype(jnp.float32) + scale_f * mixed).astype(jnp.bfloat16)
    grad_out = cotangent * land.reshape(row_count)[None, :].astype(jnp.bfloat16)
    grad_mixed = (scale_f * grad_out.astype(jnp.float32)).astype(jnp.bfloat16)
    grad_mixed_all = lax.all_gather(grad_mixed, "fsdp", axis=0, tiled=True)
    down_local = jnp.dot(grad_mixed_all, hidden, preferred_element_type=jnp.float32)
    grad_hidden = lax.dot_general(
        grad_mixed_all, down_full, (((0,), (0,)), ((), ())), preferred_element_type=jnp.float32
    )
    grad_pre = (grad_hidden * gelu_slope(pre_act)).astype(jnp.bfloat16)
    partial_grad = lax.dot_general(
        up_full, grad_pre, (((1,), (1,)), ((), ())), preferred_element_type=jnp.float32
    )
    grad_normed = lax.psum_scatter(
        partial_grad.astype(jnp.bfloat16), "fsdp", scatter_dimension=0, tiled=True
    ).astype(jnp.float32)
    up_local = jnp.dot(normed, grad_pre, preferred_element_type=jnp.float32)
    grad_centered = grad_normed * gain_f
    first_sum, second_sum = lax.psum(
        (jnp.sum(grad_centered, axis=0), jnp.sum(grad_centered * centered, axis=0)), "fsdp"
    )
    grad_conv = (
        inv_scale[None, :]
        * (
            grad_centered
            - first_sum[None, :] / full_width
            - centered * (second_sum[None, :] / full_width)
        )
    ).astype(jnp.bfloat16)
    grad_pad = depthwise_back_flat(
        grad_conv.reshape(channels, tile_count, side_len, side_len), kernel
    )
    inner = slice(3, 3 + side_len)

    def returned(face_index, grad_face):
        masked = jnp.where(masks[face_index], grad_face, 0.0).reshape(3 * channels, face_cols)
        moved = jnp.dot(
            masked,
            selectors[face_index],
            precision=lax.Precision.HIGHEST,
            preferred_element_type=jnp.float32,
        )
        return moved.reshape(3, channels, tile_count, side_len)

    tile_grad = (
        grad_out.astype(jnp.float32).reshape(channels, tile_count, side_len, side_len)
        + grad_pad[:, :, inner, inner]
    )
    edge_north = returned(0, jnp.transpose(grad_pad[:, :, 0:3, inner], (2, 0, 1, 3)))
    tile_grad = tile_grad + jnp.pad(
        jnp.transpose(edge_north, (1, 2, 0, 3)), ((0, 0), (0, 0), (side_len - 3, 0), (0, 0))
    )
    edge_south = returned(1, jnp.transpose(grad_pad[:, :, side_len + 3 :, inner], (2, 0, 1, 3)))
    tile_grad = tile_grad + jnp.pad(
        jnp.transpose(edge_south, (1, 2, 0, 3)), ((0, 0), (0, 0), (0, side_len - 3), (0, 0))
    )
    edge_west = returned(2, jnp.transpose(grad_pad[:, :, inner, 0:3], (3, 0, 1, 2)))
    edge_east = returned(3, jnp.transpose(grad_pad[:, :, inner, side_len + 3 :], (3, 0, 1, 2)))
    coming = padded_2(
        jnp.stack([edge_west, edge_east]).astype(jnp.bfloat16), (("dp", 0),), 1
    ).astype(jnp.float32)
    tile_grad = tile_grad + jnp.pad(
        jnp.transpose(coming[0], (1, 2, 3, 0)), ((0, 0), (0, 0), (0, 0), (0, side_len - 3))
    )
    tile_grad = tile_grad + jnp.pad(
        jnp.transpose(coming[3], (1, 2, 3, 0)), ((0, 0), (0, 0), (0, 0), (side_len - 3, 0))
    )
    up_grad, down_grad = (
        lax.psum_scatter(up_local, "dp", scatter_dimension=0, tiled=True),
        lax.psum_scatter(down_local, "dp", scatter_dimension=0, tiled=True),
    )
    return (
        block_out,
        tile_grad.reshape(channels, row_count).astype(jnp.bfloat16),
        up_grad,
        down_grad,
    )


def solution(mesh):
    return jax.shard_map(
        per_device,
        mesh=mesh,
        in_specs=(
            P("fsdp", "dp"),
            P(None, "fsdp"),
            P("fsdp"),
            P("dp", "fsdp"),
            P("dp", "fsdp"),
            P("fsdp"),
            P("dp", None, None),
            P("dp", None, None),
            P("dp", None),
            P("dp", None, None),
            P("fsdp", "dp"),
        ),
        out_specs=(P("fsdp", "dp"), P("fsdp", "dp"), P("dp", "fsdp"), P("dp", "fsdp")),
        check_vma=False,
    )
```

profile of v0, /device:TPU:0, one launch (start us, length us, event | category | flops | bytes accessed | tf_op | source)
XLA Modules:
  0.0 332.0 jit_solution(18306756545510592530)
XLA Ops:
  8.4 4.9 %collective-permute-start = (bf16[1,3,192,8,8]{2,1,4,3,0:T(4,128)(2,1)S(1)}, bf16[1,3,192,8,8]{2,1,4,3,0:T(4,128)(2,1)S(1)}, u32[]{:S(2)}, u32[]{:S(2)}) collective-permute-start(bf16[1,3,192,8,8]{2,1,4,3,0:T(4,128)(2,1)S(1)} %get-tuple-element.40), channel_id=1, source_target_pairs={{0,4},{4,8},{8,12},{12,16},{16,20},{20,24},{24,28},{1,5},{5,9},{9,... | collective-permute-start | bytes 221192 | tf_op jit(solution)/shard_map/ppermute | solution.py:17
  13.3 1.3 collective-permute-start.1
  14.6 1.7 fusion.71
  16.3 1.7 fusion.70
  22.7 34.1 %all_gather.13 = bf16[768,384]{1,0:T(8,128)(2,1)S(1)} all-gather(bf16[96,384]{1,0:T(8,128)(2,1)S(1)} %copy-done.11), channel_id=1, replica_groups=mesh['dp'=8,'fsdp'=4] {'dp'}, dimensions={0}, use_global_device_ids=true | all-gather | bytes 663552 | tf_op jit(solution)/shard_map/all_gather | solution.py:144
  56.8 31.4 %all_gather.14 = bf16[768,384]{1,0:T(8,128)(2,1)S(1)} all-gather(bf16[96,384]{1,0:T(8,128)(2,1)S(1)} %copy-done.12), channel_id=1, replica_groups=mesh['dp'=8,'fsdp'=4] {'dp'}, dimensions={0}, use_global_device_ids=true | all-gather | bytes 663552 | tf_op jit(solution)/shard_map/all_gather | solution.py:145
  93.4 15.4 %add_convert_fusion = bf16[192,1568]{0,1:T(8,128)(2,1)S(1)} fusion(bf16[192,1568]{0,1:T(8,128)(2,1)S(1)} %reshape.685, f32[192]{0:T(256)S(1)} %bitcast.448, f32[192]{0:T(256)S(1)} %bitcast.446, f32[192]{0:T(256)S(1)} %bitcast.444, f32[192]{0:T(256)S(1)} %bitcast.442, f32[192]{0:T(256)S(1)} %bitcast.440, f32[192]{0:T(256)S(1)} %bitcast.438, ...), kind=kLoop, calls=%fused_computation.4 | loop fusion | flops 44255232 | bytes 1241856 | tf_op jit(solution)/shard_map/convert.9
  109.3 5.7 %all-reduce.8 = (f32[512]{0:T(512)S(1)}, f32[512]{0:T(512)S(1)}) all-reduce(f32[512]{0:T(512)S(1)} %get-tuple-element.27, f32[512]{0:T(512)S(1)} %get-tuple-element.26), channel_id=1, replica_groups=mesh['dp'=8,'fsdp'=4] {'fsdp'}, use_global_device_ids=true, to_apply=%region_3.4 | all-reduce | flops 1024 | bytes 8192 | tf_op jit(solution)/shard_map/psum | solution.py:159
  115.3 8.8 %all_gather.12 = bf16[768,512]{1,0:T(8,128)(2,1)S(1)} all-gather(bf16[192,512]{1,0:T(8,128)(2,1)S(1)} %copy.119), channel_id=1, replica_groups=mesh['dp'=8,'fsdp'=4] {'fsdp'}, dimensions={0}, use_global_device_ids=true | all-gather | bytes 983040 | tf_op jit(solution)/shard_map/all_gather | solution.py:165
  124.1 1.5 multiply_convert_fusion
  127.1 1.2 copy.138
  128.5 22.6 %reduce-scatter.13.cloned.1.call-done = bf16[192,512]{1,0:T(8,128)(2,1)} async-done(((bf16[768,512]{1,0:T(8,128)(2,1)}), bf16[192,512]{1,0:T(8,128)(2,1)}) %reduce-scatter.13.cloned.1.call-update) | async-done | bytes 196624 | tf_op jit(solution)/shard_map/reduce_scatter | solution.py:173
  151.1 1.8 multiply_convert_fusion.1
  152.9 8.0 %all_gather.15 = bf16[768,512]{1,0:T(8,128)(2,1)S(1)} all-gather(bf16[192,512]{1,0:T(8,128)(2,1)S(1)} %get-tuple-element.105), channel_id=1, replica_groups=mesh['dp'=8,'fsdp'=4] {'fsdp'}, dimensions={0}, use_global_device_ids=true | all-gather | bytes 983040 | tf_op jit(solution)/shard_map/all_gather | solution.py:180
  164.5 1.6 fusion.82
  167.2 1.6 fusion.81
  168.8 19.3 %reduce-scatter.15.cloned.1.call-done = bf16[192,512]{1,0:T(8,128)(2,1)} async-done(((bf16[768,512]{1,0:T(8,128)(2,1)}), bf16[192,512]{1,0:T(8,128)(2,1)}) %reduce-scatter.15.cloned.1.call-update) | async-done | bytes 196624
  189.6 5.8 %all-reduce.7 = (f32[512]{0:T(512)S(1)}, f32[512]{0:T(512)S(1)}) all-reduce(f32[512]{0:T(512)S(1)} %get-tuple-element.25, f32[512]{0:T(512)S(1)} %get-tuple-element.24), channel_id=1, replica_groups=mesh['dp'=8,'fsdp'=4] {'fsdp'}, use_global_device_ids=true, to_apply=%region_9.10 | all-reduce | flops 1024 | bytes 8192 | tf_op jit(solution)/shard_map/psum | solution.py:194
  196.1 15.4 %multiply_add_fusion = f32[192,1568]{0,1:T(8,128)S(1)} fusion(f32[192,1568]{0,1:T(8,128)S(1)} %reshape.694, f32[192]{0:T(256)} %bitcast.449, f32[192]{0:T(256)} %bitcast.447, f32[192]{0:T(256)} %bitcast.445, f32[192]{0:T(256)} %bitcast.443, f32[192]{0:T(256)} %bitcast.441, f32[192]{0:T(256)} %bitcast.439, f32[192]{0:T(256)} %bitcast.437, f32[192]{0:T(256)} %bitcast.435, ...), kind=kLoop, calls=%fused_computation | loop fusion | flops 29202432 | bytes 2446080 | tf_op jit(solution)/shard_map/add | solution.py:78
  212.9 1.3 collective-permute-start.3
  214.2 4.6 %collective-permute-start.2 = (bf16[1,3,192,8,8]{2,1,3,4,0:T(4,128)(2,1)S(1)}, bf16[1,3,192,8,8]{2,1,3,4,0:T(4,128)(2,1)S(1)}, u32[]{:S(2)}, u32[]{:S(2)}) collective-permute-start(bf16[1,3,192,8,8]{2,1,3,4,0:T(4,128)(2,1)S(1)} %bitcast.348), channel_id=1, source_target_pairs={{0,4},{4,8},{8,12},{12,16},{16,20},{20,24},{24,28},{1,5},{5,9},{9,... | collective-permute-start | bytes 221192 | tf_op jit(solution)/shard_map/ppermute | solution.py:17
  220.2 4.4 %collective-permute-done.2 = bf16[1,3,192,8,8]{2,1,3,4,0:T(4,128)(2,1)S(1)} collective-permute-done((bf16[1,3,192,8,8]{2,1,3,4,0:T(4,128)(2,1)S(1)}, bf16[1,3,192,8,8]{2,1,3,4,0:T(4,128)(2,1)S(1)}, u32[]{:S(2)}, u32[]{:S(2)}) %collective-permute-start.2) | collective-permute-done | bytes 73760 | tf_op jit(solution)/shard_map/ppermute | solution.py:17
  225.9 31.9 %reduce-scatter.11.cloned.1.call-done = f32[96,384]{1,0:T(8,128)} async-done(((f32[768,384]{1,0:T(8,128)}), f32[96,384]{1,0:T(8,128)}) %reduce-scatter.11.cloned.1.call-update) | async-done | bytes 147472 | tf_op jit(solution)/shard_map/reduce_scatter | solution.py:245
  257.7 67.7 %reduce-scatter.9.cloned.1.call-done = f32[96,384]{1,0:T(8,128)} async-done(((f32[768,384]{1,0:T(8,128)}), f32[96,384]{1,0:T(8,128)}) %reduce-scatter.9.cloned.1.call-update) | async-done | bytes 147472 | tf_op jit(solution)/shard_map/reduce_scatter | solution.py:244
  (249 shorter events, 23.2 us)
Async XLA Ops:
  7.2 143.9 %reduce-scatter.13.cloned.1.call-start = ((), (), s32[]{:S(2)}) async-start(), calls=%async_computation.6 | async-start | bytes 983040 | tf_op jit(solution)/shard_map/reduce_scatter | solution.py:173
  8.4 81.8 %collective-permute-start = (bf16[1,3,192,8,8]{2,1,4,3,0:T(4,128)(2,1)S(1)}, bf16[1,3,192,8,8]{2,1,4,3,0:T(4,128)(2,1)S(1)}, u32[]{:S(2)}, u32[]{:S(2)}) collective-permute-start(bf16[1,3,192,8,8]{2,1,4,3,0:T(4,128)(2,1)S(1)} %get-tuple-element.40), channel_id=1, source_target_pairs={{0,4},{4,8},{8,12},{12,16},{16,20},{20,24},{24,28},{1,5},{5,9},{9,... | collective-permute-start | bytes 221192 | tf_op jit(solution)/shard_map/ppermute | solution.py:17
  13.3 77.5 %collective-permute-start.1 = (bf16[1,3,192,8,8]{2,1,4,3,0:T(4,128)(2,1)S(1)}, bf16[1,3,192,8,8]{2,1,4,3,0:T(4,128)(2,1)S(1)}, u32[]{:S(2)}, u32[]{:S(2)}) collective-permute-start(bf16[1,3,192,8,8]{2,1,4,3,0:T(4,128)(2,1)S(1)} %get-tuple-element.41), channel_id=1, source_target_pairs={{4,0},{8,4},{12,8},{16,12},{20,16},{24,20},{28,24},{5,1},{9,5},{13... | collective-permute-start | bytes 221192 | tf_op jit(solution)/shard_map/ppermute | solution.py:20
  18.0 4.7 %copy-start.11 = (bf16[96,384]{1,0:T(8,128)(2,1)S(1)}, bf16[96,384]{1,0:T(8,128)(2,1)}, u32[]{:S(2)}) copy-start(bf16[96,384]{1,0:T(8,128)(2,1)} %param.14) | copy-start | bytes 221188
  21.3 35.6 %copy-start.12 = (bf16[96,384]{1,0:T(8,128)(2,1)S(1)}, bf16[96,384]{1,0:T(8,128)(2,1)}, u32[]{:S(2)}) copy-start(bf16[96,384]{1,0:T(8,128)(2,1)} %param.15) | copy-start | bytes 221188
  21.7 66.7 %copy-start.9 = (f32[64,64]{0,1:T(8,128)}, f32[64,64]{0,1:T(8,128)S(1)}, u32[]{:S(2)}) copy-start(f32[64,64]{0,1:T(8,128)S(1)} %add.581) | copy-start | bytes 49156
  22.2 67.6 %copy-start.63 = (bf16[192]{0:T(256)(128)(2,1)S(1)}, bf16[192]{0:T(256)(128)(2,1)}, u32[]{:S(2)}) copy-start(bf16[192]{0:T(256)(128)(2,1)} %param.13) | copy-start | bytes 1156
  88.2 37.5 %copy-start = (bf16[768,384]{1,0:T(8,128)(2,1)}, bf16[768,384]{1,0:T(8,128)(2,1)S(1)}, u32[]{:S(2)}) copy-start(bf16[768,384]{1,0:T(8,128)(2,1)S(1)} %all_gather.14) | copy-start | bytes 1769476
  89.8 3.1 copy-start.52
  89.8 3.1 copy-start.53
  89.8 3.1 copy-start.54
  89.8 3.1 copy-start.55
  89.9 3.1 copy-start.56
  127.1 24.0 %copy-start.7 = (bf16[192,512]{1,0:T(8,128)(2,1)S(1)}, bf16[192,512]{1,0:T(8,128)(2,1)}, u32[]{:S(2)}) copy-start(bf16[192,512]{1,0:T(8,128)(2,1)} %param.11) | copy-start | bytes 589828
  127.1 24.0 %copy-start.8 = (bf16[192,512]{1,0:T(8,128)(2,1)S(1)}, bf16[192,512]{1,0:T(8,128)(2,1)}, u32[]{:S(2)}) copy-start(bf16[192,512]{1,0:T(8,128)(2,1)} %param.21) | copy-start | bytes 589828
  128.3 32.7 %copy-start.1 = (bf16[768,384]{1,0:T(8,128)(2,1)S(1)}, bf16[768,384]{1,0:T(8,128)(2,1)}, u32[]{:S(2)}) copy-start(bf16[768,384]{1,0:T(8,128)(2,1)} %copy-done) | copy-start | bytes 1769476
  128.3 59.8 %reduce-scatter.15.cloned.1.call-start = ((), (), s32[]{:S(2)}) async-start(), calls=%async_computation.7 | async-start | bytes 983040
  151.1 9.8 %copy-start.65 = (f32[512,384]{1,0:T(8,128)S(1)}, f32[512,384]{1,0:T(8,128)}, u32[]{:S(2)}) copy-start(f32[512,384]{1,0:T(8,128)} %get-tuple-element.128) | copy-start | bytes 2359300
  164.2 93.5 %reduce-scatter.11.cloned.1.call-start = ((), (), s32[]{:S(2)}) async-start(), calls=%async_computation.5 | async-start | bytes 1327104 | tf_op jit(solution)/shard_map/reduce_scatter | solution.py:245
  166.1 159.3 %reduce-scatter.9.cloned.1.call-start = ((), (), s32[]{:S(2)}) async-start(), calls=%async_computation.4 | async-start | bytes 1327104 | tf_op jit(solution)/shard_map/reduce_scatter | solution.py:244
  211.7 7.5 %copy-start.10 = (f32[64,64]{0,1:T(8,128)S(1)}, f32[64,64]{0,1:T(8,128)}, u32[]{:S(2)}) copy-start(f32[64,64]{0,1:T(8,128)} %copy-done.9) | copy-start | bytes 49156
  212.4 12.4 %copy-start.2 = (f32[192,512]{0,1:T(8,128)S(1)}, f32[192,512]{0,1:T(8,128)}, u32[]{:S(2)}) copy-start(f32[192,512]{0,1:T(8,128)} %copy.121) | copy-start | bytes 1179652
  212.9 7.3 %collective-permute-start.3 = (bf16[1,3,192,8,8]{2,1,3,4,0:T(4,128)(2,1)S(1)}, bf16[1,3,192,8,8]{2,1,3,4,0:T(4,128)(2,1)S(1)}, u32[]{:S(2)}, u32[]{:S(2)}) collective-permute-start(bf16[1,3,192,8,8]{2,1,3,4,0:T(4,128)(2,1)S(1)} %bitcast.350), channel_id=1, source_target_pairs={{4,0},{8,4},{12,8},{16,12},{20,16},{24,20},{28,24},{5,1},{9,5},{13... | collective-permute-start | bytes 221192 | tf_op jit(solution)/shard_map/ppermute | solution.py:20
  214.2 10.4 %collective-permute-start.2 = (bf16[1,3,192,8,8]{2,1,3,4,0:T(4,128)(2,1)S(1)}, bf16[1,3,192,8,8]{2,1,3,4,0:T(4,128)(2,1)S(1)}, u32[]{:S(2)}, u32[]{:S(2)}) collective-permute-start(bf16[1,3,192,8,8]{2,1,3,4,0:T(4,128)(2,1)S(1)} %bitcast.348), channel_id=1, source_target_pairs={{0,4},{4,8},{8,12},{12,16},{16,20},{20,24},{24,28},{1,5},{5,9},{9,... | collective-permute-start | bytes 221192 | tf_op jit(solution)/shard_map/ppermute | solution.py:17
  (50 other events, 82.9 us)
Sparse Core Ops, SparseCore 0:
  128.4 22.6 reduce-scatter.12
  164.4 23.7 reduce-scatter.14
  192.1 65.5 reduce-scatter.10
  261.5 63.8 reduce-scatter.8
where the time goes:
time: 333 us; the launch traced here: 332 us
  waiting for transfers between devices  147 us (44%)
  blocking collectives  93.8 us (28%)
  other arithmetic  36.9 us (11%)
  local copies, waits for them, and re-layouts  18.2 us (5%)
  between operations  15.3 us (5%)
  starting transfers between devices  12.4 us (4%)
  matrix products  8.83 us (3%)
    reduce_scatter x1, waiting for transfers between devices, per_device(): lax.psum_scatter(up_local, 'dp', scatter_dimension=0, tiled=True)  67.7 us
    all_gather x1, blocking collectives, per_device(): lax.all_gather(w_up, 'dp', axis=0, tiled=True)  34.1 us
    reduce_scatter x1, waiting for transfers between devices, per_device(): lax.psum_scatter(down_local, 'dp', scatter_dimension=0, tiled=True)  31.9 us
    all_gather x1, blocking collectives, per_device(): lax.all_gather(w_down, 'dp', axis=0, tiled=True)  31.4 us
    reduce_scatter x1, waiting for transfers between devices, per_device(): lax.psum_scatter(partial_out.astype(jnp.bfloat16), 'fsdp', scatter_dimens...  22.6 us
    unnamed x5, waiting for transfers between devices  19.4 us
    add x1, other arithmetic, depthwise_back_flat(): summed + placed[:, lead - offset:lead - offset + total] * taps[row_tap *...  15.4 us
    another operation x1, other arithmetic  15.4 us
  transfers between devices with their start and end apart: 8, of which 6 were waited for; matrix products, arithmetic and copies ran while one was open for 11% of the time, Pallas kernels for 0%

commit v1 on v0

v1 whole, which is shorter than its diff:
```python
import math

import jax
import jax.numpy as jnp
from jax import lax
from jax.experimental import pallas as pl
from jax.experimental.pallas import tpu as pltpu
from jax.sharding import PartitionSpec as P

root_half = 1.0 / math.sqrt(2.0)
root_tau = 1.0 / math.sqrt(2.0 * math.pi)
LAYERS = 3
KSIZE = 7
F32 = jnp.float32
BF16 = jnp.bfloat16

ROWS_LANES = (((1,), (1,)), ((), ()))
ROWS_ROWS = (((0,), (0,)), ((), ()))


def dot(a, b, dims):
    return lax.dot_general(a, b, dims, preferred_element_type=F32)


def gelu_value(hidden):
    return 0.5 * hidden * (1.0 + jax.scipy.special.erf(hidden * root_half))


def gelu_slope(hidden):
    return (
        0.5 * (1.0 + jax.scipy.special.erf(hidden * root_half))
        + hidden * jnp.exp(-0.5 * hidden * hidden) * root_tau
    )


def one_hot(target, width):
    groups, tile_count, _ = target.shape
    col = lax.broadcasted_iota(jnp.int32, (groups, tile_count, width), 2)
    hit = jnp.where(col == target, 1.0, 0.0)
    return hit.reshape(groups * tile_count, width)


def cell_order(side, tile_count):
    cells = side * side
    shape = (cells, tile_count, cells * tile_count)
    target = lax.broadcasted_iota(jnp.int32, shape, 1) * cells + lax.broadcasted_iota(
        jnp.int32, shape, 0
    )
    return one_hot(target, shape[2]).astype(BF16)


def edge_order(side, tile_count, first):
    cells = side * side
    width = cells * tile_count
    parts = []
    for layer in range(LAYERS):
        shape = (side, tile_count, width)
        target = (
            lax.broadcasted_iota(jnp.int32, shape, 1) * cells
            + lax.broadcasted_iota(jnp.int32, shape, 0) * side
            + (first + layer)
        )
        parts.append(one_hot(target, width))
    return jnp.concatenate(parts, axis=0).astype(BF16)


def by_tile(table, tile_count, width, pick):
    row = lax.broadcasted_iota(jnp.int32, (tile_count, width), 0)
    out = jnp.zeros((tile_count, width), jnp.int32)
    for tile in range(tile_count):
        out = jnp.where(row == tile, pick(table, tile), out)
    return out


def selector(nb, sh, hw, face, side, tile_count):
    cells = side * side
    vertical = face < 2
    width = cells * tile_count if vertical else LAYERS * side * tile_count
    far_first = face in (0, 2)
    widths = by_tile(hw, tile_count, width, lambda ref, t: ref[t, face])
    slots = []
    moves = []
    for entry in range(2):
        slots.append(
            by_tile(
                nb,
                tile_count,
                width,
                lambda ref, t: jnp.where(
                    ref[t, face, entry] >= 0, lax.rem(ref[t, face, entry], tile_count), -1
                ),
            )
        )
        moves.append(by_tile(sh, tile_count, width, lambda ref, t: ref[t, face, entry]))
    col = lax.broadcasted_iota(jnp.int32, (tile_count, width), 1)

    def block(layer, position):
        keep = widths >= (LAYERS - layer if far_first else layer + 1)
        total = jnp.zeros((tile_count, width), F32)
        for slot, move in zip(slots, moves):
            along = move + position
            good = keep & (slot >= 0) & (along >= 0) & (along < side)
            if vertical:
                row = side - LAYERS + layer if far_first else layer
                target = slot * cells + row * side + along
            else:
                target = layer * (side * tile_count) + along * tile_count + slot
            total = total + jnp.where(good & (col == target), 1.0, 0.0)
        return total

    if vertical:
        blocks = [block(layer, p) for layer in range(LAYERS) for p in range(side)]
    else:
        blocks = [block(layer, p) for p in range(side) for layer in range(LAYERS)]
    return jnp.concatenate(blocks, axis=0).astype(BF16)


def edges_kernel(side, tile_count, x_ref, low_ref, high_ref):
    x = x_ref[...]
    low_ref[...] = dot(edge_order(side, tile_count, 0), x, ROWS_LANES).astype(BF16)
    high_ref[...] = dot(edge_order(side, tile_count, side - LAYERS), x, ROWS_LANES).astype(BF16)


def conv_kernel(
    side, tile_count, nb, sh, hw, x_ref, west_ref, east_ref, taps_ref, out_ref, pad_ref, tap_ref, row_ref
):
    channels = x_ref.shape[0]
    wide = side + 2 * LAYERS
    far = side + LAYERS
    tap_ref[...] = taps_ref[...].astype(F32)
    corner = jnp.zeros((LAYERS, LAYERS, tile_count, channels), F32)
    for top in (0, far):
        for left in (0, far):
            pad_ref[top : top + LAYERS, left : left + LAYERS] = corner
    x = x_ref[...]
    order = cell_order(side, tile_count)
    pad_ref[LAYERS:far, LAYERS:far] = dot(order, x, ROWS_LANES).reshape(
        side, side, tile_count, channels
    )

    def halo(face, source, dims):
        picked = dot(selector(nb, sh, hw, face, side, tile_count), source, dims)
        return picked.astype(BF16).astype(F32)

    across = (LAYERS, side, tile_count, channels)
    down = (side, LAYERS, tile_count, channels)
    plain = (((1,), (0,)), ((), ()))
    pad_ref[0:LAYERS, LAYERS:far] = halo(0, x, ROWS_LANES).reshape(across)
    pad_ref[far:wide, LAYERS:far] = halo(1, x, ROWS_LANES).reshape(across)
    pad_ref[LAYERS:far, 0:LAYERS] = halo(2, west_ref[...], plain).reshape(down)
    pad_ref[LAYERS:far, far:wide] = halo(3, east_ref[...], plain).reshape(down)

    def one_row(i, carry):
        acc = [jnp.zeros((tile_count, channels), F32) for _ in range(side)]
        for a in range(KSIZE):
            window = [pad_ref[i + a, j] for j in range(wide)]
            for b in range(KSIZE):
                tap = tap_ref[pl.ds(a * KSIZE + b, 1), :]
                for j in range(side):
                    acc[j] = acc[j] + window[j + b] * tap
        for j in range(side):
            row_ref[i, j] = acc[j]
        return carry

    lax.fori_loop(0, side, one_row, 0)
    rows = row_ref[...].reshape(side * side * tile_count, channels).astype(BF16)
    out_ref[...] = dot(rows, order, ROWS_ROWS).astype(BF16)


def back_kernel(
    side,
    tile_count,
    full_width,
    nb,
    sh,
    hw,
    p0_ref,
    p1_ref,
    p2_ref,
    p3_ref,
    conv_ref,
    stat_ref,
    gain_ref,
    taps_ref,
    out_grad_ref,
    main_ref,
    west_ref,
    east_ref,
    grad_ref,
    pad_ref,
    tap_ref,
):
    channels = conv_ref.shape[0]
    wide = side + 2 * LAYERS
    far = side + LAYERS
    tap_ref[...] = taps_ref[...].astype(F32)
    summed = (p0_ref[...].astype(F32) + p1_ref[...].astype(F32)) + (
        p2_ref[...].astype(F32) + p3_ref[...].astype(F32)
    )
    g = summed * gain_ref[...]
    mean, inv, first, second = (stat_ref[k : k + 1, :] for k in range(4))
    centered = (conv_ref[...].astype(F32) - mean) * inv
    grad_conv = (inv * (g - first / full_width - centered * (second / full_width))).astype(BF16)
    order = cell_order(side, tile_count)
    grad_ref[...] = dot(order, grad_conv, ROWS_LANES).reshape(side, side, tile_count, channels)

    def one_row(r, carry):
        def one_tap(a, acc):
            source = [grad_ref[r - a, j] for j in range(side)]
            acc = list(acc)
            for b in range(KSIZE):
                tap = tap_ref[pl.ds(a * KSIZE + b, 1), :]
                for j in range(side):
                    acc[j + b] = acc[j + b] + source[j] * tap
            return tuple(acc)

        low = jnp.maximum(r - (side - 1), 0)
        high = jnp.minimum(r, KSIZE - 1) + 1
        zero = tuple(jnp.zeros((tile_count, channels), F32) for _ in range(wide))
        acc = lax.fori_loop(low, high, one_tap, zero)
        for j in range(wide):
            pad_ref[r, j] = acc[j]
        return carry

    lax.fori_loop(0, wide, one_row, 0)

    def flat(part):
        return part.reshape(-1, channels)

    inner = flat(pad_ref[LAYERS:far, LAYERS:far])
    inner_top = inner.astype(BF16)
    inner_rest = (inner - inner_top.astype(F32)).astype(BF16)
    north = flat(pad_ref[0:LAYERS, LAYERS:far]).astype(BF16)
    south = flat(pad_ref[far:wide, LAYERS:far]).astype(BF16)
    west = flat(pad_ref[LAYERS:far, 0:LAYERS]).astype(BF16)
    east = flat(pad_ref[LAYERS:far, far:wide]).astype(BF16)
    west_ref[...] = dot(selector(nb, sh, hw, 2, side, tile_count), west, ROWS_ROWS).astype(BF16)
    east_ref[...] = dot(selector(nb, sh, hw, 3, side, tile_count), east, ROWS_ROWS).astype(BF16)
    main_ref[...] = (
        out_grad_ref[...].astype(F32)
        + dot(inner_top, order, ROWS_ROWS)
        + dot(inner_rest, order, ROWS_ROWS)
        + dot(north, selector(nb, sh, hw, 0, side, tile_count), ROWS_ROWS)
        + dot(south, selector(nb, sh, hw, 1, side, tile_count), ROWS_ROWS)
    )


def last_kernel(side, tile_count, main_ref, low_ref, high_ref, out_ref):
    total = (
        main_ref[...]
        + dot(low_ref[...], edge_order(side, tile_count, 0), ROWS_ROWS)
        + dot(high_ref[...], edge_order(side, tile_count, side - LAYERS), ROWS_ROWS)
    )
    out_ref[...] = total.astype(BF16)


def smem():
    return pl.BlockSpec(memory_space=pltpu.SMEM)


def vmem():
    return pl.BlockSpec(memory_space=pltpu.VMEM)


def flips(count, mask):
    return [(i, i ^ mask) for i in range(count)]


def pick(pair, index):
    return lax.dynamic_index_in_dim(pair, index, 0, keepdims=False)


def gather_rows(block, axis, masks):
    count = lax.axis_size(axis)
    place = lax.axis_index(axis)
    bits = count.bit_length() - 1
    held = block.reshape((1,) * bits + block.shape)
    for mask in masks:
        dim = bits - mask.bit_length()
        other = lax.ppermute(held, axis, flips(count, mask))
        upper = (place & mask) != 0
        held = jnp.where(
            upper,
            jnp.concatenate([other, held], axis=dim),
            jnp.concatenate([held, other], axis=dim),
        )
    return held.reshape((count * block.shape[0],) + block.shape[1:])


def scatter_rows(total, axis, masks):
    count = lax.axis_size(axis)
    place = lax.axis_index(axis)
    bits = count.bit_length() - 1
    held = total.reshape((2,) * bits + (total.shape[0] // count,) + total.shape[1:])
    for mask in masks:
        dim = bits - mask.bit_length()
        bit = jnp.where((place & mask) != 0, 1, 0)
        mine = lax.dynamic_slice_in_dim(held, bit, 1, axis=dim)
        theirs = lax.dynamic_slice_in_dim(held, 1 - bit, 1, axis=dim)
        other = lax.ppermute(theirs.astype(BF16), axis, flips(count, mask))
        held = mine + other.astype(F32)
    return held.reshape((total.shape[0] // count,) + total.shape[1:])


def per_device(
    tiles,
    kernel,
    norm_gain,
    w_up,
    w_down,
    layer_scale,
    neighbors,
    shifts,
    halo_widths,
    land,
    cotangent,
):
    channels = tiles.shape[0]
    tile_count, side = land.shape[0], land.shape[1]
    cells = tile_count * side * side
    edge_rows = LAYERS * side * tile_count
    wide = side + 2 * LAYERS
    parts = lax.axis_size("fsdp")
    here = lax.axis_index("fsdp")
    full_width = channels * parts
    dp = lax.axis_size("dp")
    forward = [(i, i + 1) for i in range(dp - 1)]
    backward = [(i + 1, i) for i in range(dp - 1)]
    shape = jax.ShapeDtypeStruct
    tables = (neighbors, shifts, halo_widths)
    edge = shape((edge_rows, channels), BF16)
    grid = shape((channels, cells), BF16)

    low, high = pl.pallas_call(
        lambda *refs: edges_kernel(side, tile_count, *refs),
        out_shape=(edge, edge),
        name="edges",
    )(tiles)
    west_src = lax.ppermute(high, "dp", forward)
    east_src = lax.ppermute(low, "dp", backward)

    grad_out = cotangent * land.reshape(cells)[None, :].astype(BF16)
    scale_f = layer_scale.astype(F32)[:, None]
    grad_mixed = (scale_f * grad_out.astype(F32)).astype(BF16)
    grad_mixed_all = lax.all_gather(grad_mixed, "fsdp", axis=0, tiled=True)
    gain_all = lax.all_gather(norm_gain, "fsdp", axis=0, tiled=True).astype(F32)[:, None]

    if dp & (dp - 1) == 0 and dp <= 16:
        masks = [1 << k for k in range(dp.bit_length() - 1)]
        up_full = gather_rows(w_up, "dp", masks[::-1])
        down_full = gather_rows(w_down, "dp", masks[:1] + masks[:0:-1])
    else:
        masks = None
        up_full = lax.all_gather(w_up, "dp", axis=0, tiled=True)
        down_full = lax.all_gather(w_down, "dp", axis=0, tiled=True)

    conv = pl.pallas_call(
        lambda *refs: conv_kernel(side, tile_count, *refs),
        out_shape=grid,
        in_specs=[smem()] * 3 + [vmem()] * 4,
        out_specs=vmem(),
        scratch_shapes=[
            pltpu.VMEM((wide, wide, tile_count, channels), F32),
            pltpu.VMEM(kernel.shape, F32),
            pltpu.VMEM((side, side, tile_count, channels), F32),
        ],
        name="conv",
    )(*tables, tiles, west_src, east_src, kernel)

    conv_all = lax.all_gather(conv, "fsdp", axis=0, tiled=True)
    values = lax.optimization_barrier(conv_all).astype(F32)
    mean = jnp.sum(values, axis=0) / full_width
    inv = lax.rsqrt(jnp.sum(values * values, axis=0) / full_width - mean * mean + 1e-06)
    centered = (values - mean[None, :]) * inv[None, :]
    normed = (centered * gain_all).astype(BF16)
    pre_act = dot(up_full, normed, ROWS_ROWS)
    hidden = gelu_value(pre_act).astype(BF16)
    grad_hidden = dot(down_full, grad_mixed_all, ROWS_ROWS)
    grad_pre = (grad_hidden * gelu_slope(pre_act)).astype(BF16)
    partial_grad = jnp.dot(up_full, grad_pre, preferred_element_type=F32).astype(BF16)
    weighted = partial_grad.astype(F32) * gain_all
    first, second = lax.psum(
        (jnp.sum(weighted, axis=0), jnp.sum(weighted * centered, axis=0)), "fsdp"
    )

    def exchange(partial):
        chunks = partial.reshape(parts, channels, cells)
        pieces = [pick(chunks, here)]
        for step in range(1, parts):
            ring = [(i, (i + step) % parts) for i in range(parts)]
            pieces.append(lax.ppermute(pick(chunks, (here + step) % parts), "fsdp", ring))
        return pieces

    down_local = dot(grad_mixed_all, hidden, ROWS_LANES)
    up_local = dot(normed, grad_pre, ROWS_LANES)
    pieces = exchange(partial_grad)
    stats = jnp.stack([mean, inv, first, second])
    main, to_west, to_east = pl.pallas_call(
        lambda *refs: back_kernel(side, tile_count, full_width, *refs),
        out_shape=(shape((channels, cells), F32), edge, edge),
        in_specs=[smem()] * 3 + [vmem()] * 9,
        out_specs=(vmem(),) * 3,
        scratch_shapes=[
            pltpu.VMEM((side, side, tile_count, channels), F32),
            pltpu.VMEM((wide, wide, tile_count, channels), F32),
            pltpu.VMEM(kernel.shape, F32),
        ],
        name="back",
    )(*tables, *pieces, conv, stats, norm_gain.astype(F32)[:, None], kernel, grad_out)
    from_east = lax.ppermute(to_west, "dp", backward)
    from_west = lax.ppermute(to_east, "dp", forward)
    tile_grad = pl.pallas_call(
        lambda *refs: last_kernel(side, tile_count, *refs),
        out_shape=grid,
        name="last",
    )(main, from_west, from_east)

    partial_out = jnp.dot(down_full, hidden, preferred_element_type=F32).astype(BF16)
    mixed = sum(piece.astype(F32) for piece in exchange(partial_out))
    block_out = (tiles.astype(F32) + scale_f * mixed).astype(BF16)

    if masks is not None:
        order = masks
        up_grad = scatter_rows(up_local, "dp", order)
        down_grad = scatter_rows(down_local, "dp", order)
    else:
        up_grad = lax.psum_scatter(up_local, "dp", scatter_dimension=0, tiled=True)
        down_grad = lax.psum_scatter(down_local, "dp", scatter_dimension=0, tiled=True)
    return block_out, tile_grad, up_grad, down_grad


def solution(mesh):
    return jax.shard_map(
        per_device,
        mesh=mesh,
        in_specs=(
            P("fsdp", "dp"),
            P(None, "fsdp"),
            P("fsdp"),
            P("dp", "fsdp"),
            P("dp", "fsdp"),
            P("fsdp"),
            P("dp", None, None),
            P("dp", None, None),
            P("dp", None),
            P("dp", None, None),
            P("fsdp", "dp"),
        ),
        out_specs=(P("fsdp", "dp"), P("fsdp", "dp"), P("dp", "fsdp"), P("dp", "fsdp")),
        check_vma=False,
    )
```

time: 333 us -> 135 us (0.41)
  waiting for transfers between devices: 147 us -> 28.8 us
  blocking collectives: 93.8 us -> 32.2 us
  other arithmetic: 36.9 us -> 7.71 us
  starting transfers between devices: 12.4 us -> 34.8 us
  Pallas kernels: 0 us -> 15.5 us
  between operations: 15.3 us -> 1.62 us
  local copies, waits for them, and re-layouts: 18.2 us -> 9.42 us
  matrix products: 8.83 us -> 3.75 us
    reduce_scatter x3 -> x0, waiting for transfers between devices: 122 us -> none  [the longest x1 67.7 us: per_device(): lax.psum_scatter(up_local, 'dp', scatter_dimension=0, tiled=True)]
    all_gather x3 -> x1, blocking collectives: 74.3 us -> 9.16 us  [per_device(): conv_all = lax.all_gather(conv, 'fsdp', axis=0, tiled=True)]
    ppermute x4 -> x22, waiting for transfers between devices: 5.04 us -> 28.8 us  [the longest x6 9.96 us: exchange(): lax.ppermute(pick(chunks, (here + step) % parts), 'fsdp', ring)]
    ppermute x4 -> x22, starting transfers between devices: 12 us -> 34.8 us  [the longest x6 11.3 us: gather_rows(): other = lax.ppermute(held, axis, flips(count, mask))]
    unnamed x5 -> x0, waiting for transfers between devices: 19.4 us -> none
    add x14 -> x4, other arithmetic: 16.4 us -> 0.17 us  [scatter_rows(): held = mine + other.astype(F32)]
    pallas_call x0 -> x4, Pallas kernels: none -> 15.5 us  [the longest x1 6.23 us: per_device(): pl.pallas_call(lambda *refs: back_kernel(side, tile_count, full_width, *r...]
    another operation x1, other arithmetic: 15.4 us -> 0.61 us  [per_device(): stats = jnp.stack([mean, inv, first, second])]
  transfers between devices with their start and end apart: 8 -> 22, of which waited for: 6 -> 9; matrix products, arithmetic and copies ran while one was open for 11% -> 11% of each run, Pallas kernels for 0% -> 12%
where the time goes in v1:
time: 135 us; the launch traced here: 134 us
  starting transfers between devices  34.8 us (26%)
  blocking collectives  32.2 us (24%)
  waiting for transfers between devices  28.8 us (21%)
  Pallas kernels  15.5 us (11%)
  local copies, waits for them, and re-layouts  9.42 us (7%)
  other arithmetic  7.71 us (6%)
  matrix products  3.75 us (3%)
  between operations  1.62 us (1%)
    ppermute x6, starting transfers between devices, gather_rows(): other = lax.ppermute(held, axis, flips(count, mask))  11.3 us
    ppermute x6, starting transfers between devices, scatter_rows(): other = lax.ppermute(theirs.astype(BF16), axis, flips(count, mask))  11.2 us
    ppermute x6, waiting for transfers between devices, exchange(): lax.ppermute(pick(chunks, (here + step) % parts), 'fsdp', ring)  9.96 us
    psum x1, blocking collectives, per_device(): lax.psum((jnp.sum(weighted, axis=0), jnp.sum(weighted * centered, axis=0)...  9.43 us
    all_gather x1, blocking collectives, per_device(): conv_all = lax.all_gather(conv, 'fsdp', axis=0, tiled=True)  9.16 us
    ppermute x6, waiting for transfers between devices, gather_rows(): other = lax.ppermute(held, axis, flips(count, mask))  8.52 us
    all_gather x1, blocking collectives, per_device(): grad_mixed_all = lax.all_gather(grad_mixed, 'fsdp', axis=0, tiled=True)  7.87 us
    unnamed x18, local copies, waits for them, and re-layouts  7.49 us
  transfers between devices with their start and end apart: 22, of which 9 were waited for; matrix products, arithmetic and copies ran while one was open for 11% of the time, Pallas kernels for 12%

profile of v1, /device:TPU:0, one launch (start us, length us, event | category | flops | bytes accessed | tf_op | source)
XLA Modules:
  0.0 133.8 jit_solution(11200657501015002211)
XLA Ops:
  0.6 3.1 %collective-permute-start = (bf16[1,1,1,96,384]{4,3,2,1,0:T(8,128)(2,1)}, bf16[1,1,1,96,384]{4,3,2,1,0:T(8,128)(2,1)S(1)}, u32[]{:S(2)}, u32[]{:S(2)}) collective-permute-start(bf16[1,1,1,96,384]{4,3,2,1,0:T(8,128)(2,1)} %bitcast.67), channel_id=1, source_target_pairs={{0,4},{4,0},{8,12},{12,8},{16,20},{20,16},{24,28},{28,24},{1,5},{5... | collective-permute-start | bytes 221192 | tf_op jit(solution)/shard_map/ppermute | solution.py:280
  3.7 2.6 %collective-permute-start.3 = (bf16[1,1,1,96,384]{4,3,2,1,0:T(8,128)(2,1)}, bf16[1,1,1,96,384]{4,3,2,1,0:T(8,128)(2,1)S(1)}, u32[]{:S(2)}, u32[]{:S(2)}) collective-permute-start(bf16[1,1,1,96,384]{4,3,2,1,0:T(8,128)(2,1)} %bitcast.64), channel_id=1, source_target_pairs={{0,16},{4,20},{8,24},{12,28},{16,0},{20,4},{24,8},{28,12},{1,17},{... | collective-permute-start | bytes 221192 | tf_op jit(solution)/shard_map/ppermute | solution.py:280
  6.3 1.9 %edges.1 = (bf16[192,192]{1,0:T(8,128)(2,1)}, bf16[192,192]{1,0:T(8,128)(2,1)}) custom-call(bf16[192,512]{1,0:T(8,128)(2,1)} %refs_3_.1), custom_call_target="tpu_custom_call" | custom-call | tf_op jit(solution)/shard_map/edges/pallas_call | solution.py:334
  8.2 2.4 %collective-permute-start.6 = (bf16[192,192]{1,0:T(8,128)(2,1)}, bf16[192,192]{1,0:T(8,128)(2,1)S(1)}, u32[]{:S(2)}, u32[]{:S(2)}) collective-permute-start(bf16[192,192]{1,0:T(8,128)(2,1)} %get-tuple-element.9), channel_id=1, source_target_pairs={{0,4},{4,8},{8,12},{12,16},{16,20},{20,24},{24,28},{1,5},{5,9},{9,... | collective-permute-start | bytes 221192 | tf_op jit(solution)/shard_map/ppermute | solution.py:339
  13.5 1.4 %copy.21.refs_0_ = s32[8,4,2]{2,1,0:T(4,128)} copy(s32[8,4,2]{0,2,1:T(2,128)} %param.17) | data formatting | bytes 512 | tf_op args[6]
  21.0 5.7 %all-reduce = bf16[768]{0:T(1024)(128)(2,1)S(1)} all-reduce(bf16[768]{0:T(1024)(128)(2,1)S(1)} %dynamic-update-slice), channel_id=1, replica_groups=mesh['dp'=8,'fsdp'=4] {'fsdp'}, use_global_device_ids=true, to_apply=%add | all-reduce | flops 768 | bytes 3072
  28.5 3.4 %collective-permute-start.1 = (bf16[1,1,2,96,384]{4,3,2,1,0:T(8,128)(2,1)S(1)}, bf16[1,1,2,96,384]{4,3,2,1,0:T(8,128)(2,1)S(1)}, u32[]{:S(2)}, u32[]{:S(2)}) collective-permute-start(bf16[1,1,2,96,384]{4,3,2,1,0:T(8,128)(2,1)S(1)} %maximum_select_fusion.4), channel_id=1, source_target_pairs={{0,16},{4,20},{8,24},{12,28},{16,0},{20,4},{24,8},{28,12},{1,17},{... | collective-permute-start | bytes 442376 | tf_op jit(solution)/shard_map/ppermute | solution.py:280
  32.8 1.6 %collective-permute-start.4 = (bf16[2,1,1,96,384]{4,3,2,1,0:T(8,128)(2,1)S(1)}, bf16[2,1,1,96,384]{4,3,2,1,0:T(8,128)(2,1)S(1)}, u32[]{:S(2)}, u32[]{:S(2)}) collective-permute-start(bf16[2,1,1,96,384]{4,3,2,1,0:T(8,128)(2,1)S(1)} %maximum_select_fusion.6), channel_id=1, source_target_pairs={{0,8},{4,12},{8,0},{12,4},{16,24},{20,28},{24,16},{28,20},{1,9},{5... | collective-permute-start | bytes 442376 | tf_op jit(solution)/shard_map/ppermute | solution.py:280
  35.8 5.4 %conv.1.refs_7_ = bf16[192,512]{1,0:T(8,128)(2,1)} custom-call(s32[8,4,2]{2,1,0:T(4,128)} %copy.21.refs_0_, s32[8,4,2]{2,1,0:T(4,128)} %copy.22.refs_1_, s32[8,4]{1,0:T(8,128)} %copy.23.refs_2_, bf16[192,512]{1,0:T(8,128)(2,1)} %refs_3_.1, bf16[192,192]{1,0:T(8,128)(2,1)} %copy-done.4, bf16[192,192]{1,0:T(8,128)(2,1)} %copy-done.5, bf16[49,192]{1,0:T(8,128)(2,1)} %refs_10_.1), custom_call_target="tpu_custom_call" | custom-call | tf_op jit(solution)/shard_map/conv/pallas_call | solution.py:357
  41.1 9.2 %all_gather.9 = bf16[768,512]{1,0:T(8,128)(2,1)S(1)} all-gather(bf16[192,512]{1,0:T(8,128)(2,1)} %conv.1.refs_7_), channel_id=1, replica_groups=mesh['dp'=8,'fsdp'=4] {'fsdp'}, dimensions={0}, use_global_device_ids=true | all-gather | bytes 983040 | tf_op jit(solution)/shard_map/all_gather | solution.py:370
  51.4 8.5 %collective-permute-done.5 = bf16[2,2,1,96,384]{4,3,2,1,0:T(8,128)(2,1)S(1)} collective-permute-done((bf16[2,2,1,96,384]{4,3,2,1,0:T(8,128)(2,1)S(1)}, bf16[2,2,1,96,384]{4,3,2,1,0:T(8,128)(2,1)S(1)}, u32[]{:S(2)}, u32[]{:S(2)}) %collective-permute-start.5) | collective-permute-done | bytes 294944 | tf_op jit(solution)/shard_map/ppermute | solution.py:280
  62.6 4.2 %collective-permute-done.10 = bf16[192,512]{1,0:T(8,128)(2,1)S(1)} collective-permute-done((bf16[192,512]{1,0:T(8,128)(2,1)S(1)}, bf16[192,512]{1,0:T(8,128)(2,1)S(1)}, u32[]{:S(2)}, u32[]{:S(2)}) %collective-permute-start.10) | collective-permute-done | bytes 196640 | tf_op jit(solution)/shard_map/ppermute | solution.py:391
  66.8 5.3 %collective-permute-done.9 = bf16[192,512]{1,0:T(8,128)(2,1)S(1)} collective-permute-done((bf16[192,512]{1,0:T(8,128)(2,1)S(1)}, bf16[192,512]{1,0:T(8,128)(2,1)S(1)}, u32[]{:S(2)}, u32[]{:S(2)}) %collective-permute-start.9) | collective-permute-done | bytes 196640 | tf_op jit(solution)/shard_map/ppermute | solution.py:391
  73.5 7.9 %all_gather.11 = bf16[768,512]{1,0:T(8,128)(2,1)S(1)} all-gather(bf16[192,512]{1,0:T(8,128)(2,1)S(1)} %get-tuple-element.20), channel_id=1, replica_groups=mesh['dp'=8,'fsdp'=4] {'fsdp'}, dimensions={0}, use_global_device_ids=true | all-gather | bytes 983040 | tf_op jit(solution)/shard_map/all_gather | solution.py:345
  88.5 9.4 %all-reduce.1 = (f32[1,512]{1,0:T(1,128)S(1)}, f32[1,512]{1,0:T(1,128)S(1)}) all-reduce(f32[1,512]{1,0:T(1,128)S(1)} %bitcast.76, f32[1,512]{1,0:T(1,128)S(1)} %bitcast.75), channel_id=1, replica_groups=mesh['dp'=8,'fsdp'=4] {'fsdp'}, use_global_device_ids=true, to_apply=%region_5.6 | all-reduce | flops 1024 | bytes 8192 | tf_op jit(solution)/shard_map/psum | solution.py:382
  98.6 6.2 %back.1 = (f32[192,512]{1,0:T(8,128)}, bf16[192,192]{1,0:T(8,128)(2,1)}, bf16[192,192]{1,0:T(8,128)(2,1)}) custom-call(s32[8,4,2]{2,1,0:T(4,128)} %copy.21.refs_0_, s32[8,4,2]{2,1,0:T(4,128)} %copy.22.refs_1_, s32[8,4]{1,0:T(8,128)} %copy.23.refs_2_, bf16[192,512]{1,0:T(8,128)(2,1)} %get-tuple-element.25.refs_3_, ...), custom_call_target="tpu_custom_call" | custom-call | tf_op jit(solution)/shard_map/back/pallas_call | solution.py:398
  104.8 3.4 %collective-permute-start.14 = (bf16[192,192]{1,0:T(8,128)(2,1)}, bf16[192,192]{1,0:T(8,128)(2,1)}, u32[]{:S(2)}, u32[]{:S(2)}) collective-permute-start(bf16[192,192]{1,0:T(8,128)(2,1)} %get-tuple-element.12), channel_id=1, source_target_pairs={{0,4},{4,8},{8,12},{12,16},{16,20},{20,24},{24,28},{1,5},{5,9},{9,... | collective-permute-start | bytes 221192 | tf_op jit(solution)/shard_map/ppermute | solution.py:411
  109.6 2.7 %collective-permute-start.19 = (bf16[2,2,1,96,384]{4,3,2,1,0:T(8,128)(2,1)S(1)}, bf16[2,2,1,96,384]{4,3,2,1,0:T(8,128)(2,1)S(1)}, u32[]{:S(2)}, u32[]{:S(2)}) collective-permute-start(bf16[2,2,1,96,384]{4,3,2,1,0:T(8,128)(2,1)S(1)} %dynamic-slice_convert_fusion), channel_id=1, source_target_pairs={{0,4},{4,0},{8,12},{12,8},{16,20},{20,16},{24,28},{28,24},{1,5},{5... | collective-permute-start | bytes 884744 | tf_op jit(solution)/shard_map/ppermute | solution.py:300
  112.3 3.8 %collective-permute-done.15.refs_2_ = bf16[192,192]{1,0:T(8,128)(2,1)} collective-permute-done((bf16[192,192]{1,0:T(8,128)(2,1)}, bf16[192,192]{1,0:T(8,128)(2,1)}, u32[]{:S(2)}, u32[]{:S(2)}) %collective-permute-start.15) | collective-permute-done | bytes 73760 | tf_op jit(solution)/shard_map/ppermute | solution.py:410
  116.1 2.1 %last.1 = bf16[192,512]{1,0:T(8,128)(2,1)} custom-call(f32[192,512]{1,0:T(8,128)} %get-tuple-element.11.refs_0_, bf16[192,192]{1,0:T(8,128)(2,1)} %collective-permute-done.14.refs_1_, bf16[192,192]{1,0:T(8,128)(2,1)} %collective-permute-done.15.refs_2_), custom_call_target="tpu_custom_call" | custom-call | tf_op jit(solution)/shard_map/last/pallas_call | solution.py:412
  121.5 3.0 %collective-permute-done.17 = bf16[2,1,1,96,384]{4,3,2,1,0:T(8,128)(2,1)S(1)} collective-permute-done((bf16[2,1,1,96,384]{4,3,2,1,0:T(8,128)(2,1)S(1)}, bf16[2,1,1,96,384]{4,3,2,1,0:T(8,128)(2,1)S(1)}, u32[]{:S(2)}, u32[]{:S(2)}) %collective-permute-start.17) | collective-permute-done | bytes 147488 | tf_op jit(solution)/shard_map/ppermute | solution.py:300
  124.5 1.9 %collective-permute-start.18 = (bf16[1,1,1,96,384]{4,3,2,1,0:T(8,128)(2,1)S(1)}, bf16[1,1,1,96,384]{4,3,2,1,0:T(8,128)(2,1)S(1)}, u32[]{:S(2)}, u32[]{:S(2)}) collective-permute-start(bf16[1,1,1,96,384]{4,3,2,1,0:T(8,128)(2,1)S(1)} %dynamic-slice_convert_fusion.5), channel_id=1, source_target_pairs={{0,16},{4,20},{8,24},{12,28},{16,0},{20,4},{24,8},{28,12},{1,17},{... | collective-permute-start | bytes 221192 | tf_op jit(solution)/shard_map/ppermute | solution.py:300
  126.5 3.0 %collective-permute-start.21 = (bf16[1,1,1,96,384]{4,3,2,1,0:T(8,128)(2,1)S(1)}, bf16[1,1,1,96,384]{4,3,2,1,0:T(8,128)(2,1)S(1)}, u32[]{:S(2)}, u32[]{:S(2)}) collective-permute-start(bf16[1,1,1,96,384]{4,3,2,1,0:T(8,128)(2,1)S(1)} %dynamic-slice_convert_fusion.4), channel_id=1, source_target_pairs={{0,16},{4,20},{8,24},{12,28},{16,0},{20,4},{24,8},{28,12},{1,17},{... | collective-permute-start | bytes 221192 | tf_op jit(solution)/shard_map/ppermute | solution.py:300
  129.5 2.0 %collective-permute-done.18 = bf16[1,1,1,96,384]{4,3,2,1,0:T(8,128)(2,1)S(1)} collective-permute-done((bf16[1,1,1,96,384]{4,3,2,1,0:T(8,128)(2,1)S(1)}, bf16[1,1,1,96,384]{4,3,2,1,0:T(8,128)(2,1)S(1)}, u32[]{:S(2)}, u32[]{:S(2)}) %collective-permute-start.18) | collective-permute-done | bytes 73760 | tf_op jit(solution)/shard_map/ppermute | solution.py:300
  (85 shorter events, 32.1 us)
Async XLA Ops:
  0.6 26.9 %collective-permute-start = (bf16[1,1,1,96,384]{4,3,2,1,0:T(8,128)(2,1)}, bf16[1,1,1,96,384]{4,3,2,1,0:T(8,128)(2,1)S(1)}, u32[]{:S(2)}, u32[]{:S(2)}) collective-permute-start(bf16[1,1,1,96,384]{4,3,2,1,0:T(8,128)(2,1)} %bitcast.67), channel_id=1, source_target_pairs={{0,4},{4,0},{8,12},{12,8},{16,20},{20,16},{24,28},{28,24},{1,5},{5... | collective-permute-start | bytes 221192 | tf_op jit(solution)/shard_map/ppermute | solution.py:280
  3.7 28.1 %collective-permute-start.3 = (bf16[1,1,1,96,384]{4,3,2,1,0:T(8,128)(2,1)}, bf16[1,1,1,96,384]{4,3,2,1,0:T(8,128)(2,1)S(1)}, u32[]{:S(2)}, u32[]{:S(2)}) collective-permute-start(bf16[1,1,1,96,384]{4,3,2,1,0:T(8,128)(2,1)} %bitcast.64), channel_id=1, source_target_pairs={{0,16},{4,20},{8,24},{12,28},{16,0},{20,4},{24,8},{28,12},{1,17},{... | collective-permute-start | bytes 221192 | tf_op jit(solution)/shard_map/ppermute | solution.py:280
  8.2 26.3 %collective-permute-start.6 = (bf16[192,192]{1,0:T(8,128)(2,1)}, bf16[192,192]{1,0:T(8,128)(2,1)S(1)}, u32[]{:S(2)}, u32[]{:S(2)}) collective-permute-start(bf16[192,192]{1,0:T(8,128)(2,1)} %get-tuple-element.9), channel_id=1, source_target_pairs={{0,4},{4,8},{8,12},{12,16},{16,20},{20,24},{24,28},{1,5},{5,9},{9,... | collective-permute-start | bytes 221192 | tf_op jit(solution)/shard_map/ppermute | solution.py:339
  10.6 23.9 %collective-permute-start.7 = (bf16[192,192]{1,0:T(8,128)(2,1)}, bf16[192,192]{1,0:T(8,128)(2,1)S(1)}, u32[]{:S(2)}, u32[]{:S(2)}) collective-permute-start(bf16[192,192]{1,0:T(8,128)(2,1)} %get-tuple-element.10), channel_id=1, source_target_pairs={{4,0},{8,4},{12,8},{16,12},{20,16},{24,20},{28,24},{5,1},{9,5},{13... | collective-permute-start | bytes 221192 | tf_op jit(solution)/shard_map/ppermute | solution.py:340
  26.7 23.6 %copy-start.1 = (bf16[96,384]{1,0:T(8,128)(2,1)S(1)}, bf16[96,384]{1,0:T(8,128)(2,1)}, u32[]{:S(2)}) copy-start(bf16[96,384]{1,0:T(8,128)(2,1)} %param.14) | copy-start | bytes 221188
  28.5 22.3 %collective-permute-start.1 = (bf16[1,1,2,96,384]{4,3,2,1,0:T(8,128)(2,1)S(1)}, bf16[1,1,2,96,384]{4,3,2,1,0:T(8,128)(2,1)S(1)}, u32[]{:S(2)}, u32[]{:S(2)}) collective-permute-start(bf16[1,1,2,96,384]{4,3,2,1,0:T(8,128)(2,1)S(1)} %maximum_select_fusion.4), channel_id=1, source_target_pairs={{0,16},{4,20},{8,24},{12,28},{16,0},{20,4},{24,8},{28,12},{1,17},{... | collective-permute-start | bytes 442376 | tf_op jit(solution)/shard_map/ppermute | solution.py:280
  32.8 17.8 %collective-permute-start.4 = (bf16[2,1,1,96,384]{4,3,2,1,0:T(8,128)(2,1)S(1)}, bf16[2,1,1,96,384]{4,3,2,1,0:T(8,128)(2,1)S(1)}, u32[]{:S(2)}, u32[]{:S(2)}) collective-permute-start(bf16[2,1,1,96,384]{4,3,2,1,0:T(8,128)(2,1)S(1)} %maximum_select_fusion.6), channel_id=1, source_target_pairs={{0,8},{4,12},{8,0},{12,4},{16,24},{20,28},{24,16},{28,20},{1,9},{5... | collective-permute-start | bytes 442376 | tf_op jit(solution)/shard_map/ppermute | solution.py:280
  50.6 9.3 %collective-permute-start.5 = (bf16[2,2,1,96,384]{4,3,2,1,0:T(8,128)(2,1)S(1)}, bf16[2,2,1,96,384]{4,3,2,1,0:T(8,128)(2,1)S(1)}, u32[]{:S(2)}, u32[]{:S(2)}) collective-permute-start(bf16[2,2,1,96,384]{4,3,2,1,0:T(8,128)(2,1)S(1)} %maximum_select_fusion.3), channel_id=1, source_target_pairs={{0,4},{4,0},{8,12},{12,8},{16,20},{20,16},{24,28},{28,24},{1,5},{5... | collective-permute-start | bytes 884744 | tf_op jit(solution)/shard_map/ppermute | solution.py:280
  50.8 9.8 %collective-permute-start.2 = (bf16[2,1,2,96,384]{4,3,2,1,0:T(8,128)(2,1)S(1)}, bf16[2,1,2,96,384]{4,3,2,1,0:T(8,128)(2,1)S(1)}, u32[]{:S(2)}, u32[]{:S(2)}) collective-permute-start(bf16[2,1,2,96,384]{4,3,2,1,0:T(8,128)(2,1)S(1)} %maximum_select_fusion.2), channel_id=1, source_target_pairs={{0,8},{4,12},{8,0},{12,4},{16,24},{20,28},{24,16},{28,20},{1,9},{5... | collective-permute-start | bytes 884744 | tf_op jit(solution)/shard_map/ppermute | solution.py:280
  60.8 11.8 %copy-start = (bf16[192,512]{1,0:T(8,128)(2,1)S(1)}, bf16[192,512]{1,0:T(8,128)(2,1)}, u32[]{:S(2)}) copy-start(bf16[192,512]{1,0:T(8,128)(2,1)} %refs_3_.1) | copy-start | bytes 589828
  61.4 5.4 %collective-permute-start.10 = (bf16[192,512]{1,0:T(8,128)(2,1)S(1)}, bf16[192,512]{1,0:T(8,128)(2,1)S(1)}, u32[]{:S(2)}, u32[]{:S(2)}) collective-permute-start(bf16[192,512]{1,0:T(8,128)(2,1)S(1)} %get-tuple-element.27), channel_id=1, source_target_pairs={{0,3},{1,0},{2,1},{3,2},{4,7},{5,4},{6,5},{7,6},{8,11},{9,8},{10,9... | collective-permute-start | bytes 589832 | tf_op jit(solution)/shard_map/ppermute | solution.py:391
  61.5 10.6 %collective-permute-start.9 = (bf16[192,512]{1,0:T(8,128)(2,1)S(1)}, bf16[192,512]{1,0:T(8,128)(2,1)S(1)}, u32[]{:S(2)}, u32[]{:S(2)}) collective-permute-start(bf16[192,512]{1,0:T(8,128)(2,1)S(1)} %get-tuple-element.28), channel_id=1, source_target_pairs={{0,2},{1,3},{2,0},{3,1},{4,6},{5,7},{6,4},{7,5},{8,10},{9,11},{10,... | collective-permute-start | bytes 589832 | tf_op jit(solution)/shard_map/ppermute | solution.py:391
  62.6 10.0 %collective-permute-start.8 = (bf16[192,512]{1,0:T(8,128)(2,1)S(1)}, bf16[192,512]{1,0:T(8,128)(2,1)S(1)}, u32[]{:S(2)}, u32[]{:S(2)}) collective-permute-start(bf16[192,512]{1,0:T(8,128)(2,1)S(1)} %get-tuple-element.26), channel_id=1, source_target_pairs={{0,1},{1,2},{2,3},{3,0},{4,5},{5,6},{6,7},{7,4},{8,9},{9,10},{10,1... | collective-permute-start | bytes 589832 | tf_op jit(solution)/shard_map/ppermute | solution.py:391
  84.2 14.4 %collective-permute-start.11 = (bf16[192,512]{1,0:T(8,128)(2,1)}, bf16[192,512]{1,0:T(8,128)(2,1)}, u32[]{:S(2)}, u32[]{:S(2)}) collective-permute-start(bf16[192,512]{1,0:T(8,128)(2,1)} %get-tuple-element.24), channel_id=1, source_target_pairs={{0,1},{1,2},{2,3},{3,0},{4,5},{5,6},{6,7},{7,4},{8,9},{9,10},{10,1... | collective-permute-start | bytes 589832 | tf_op jit(solution)/shard_map/ppermute | solution.py:391
  84.6 14.0 %collective-permute-start.12 = (bf16[192,512]{1,0:T(8,128)(2,1)S(1)}, bf16[192,512]{1,0:T(8,128)(2,1)}, u32[]{:S(2)}, u32[]{:S(2)}) collective-permute-start(bf16[192,512]{1,0:T(8,128)(2,1)S(1)} %get-tuple-element.23), channel_id=1, source_target_pairs={{0,2},{1,3},{2,0},{3,1},{4,6},{5,7},{6,4},{7,5},{8,10},{9,11},{10,... | collective-permute-start | bytes 589832 | tf_op jit(solution)/shard_map/ppermute | solution.py:391
  85.8 12.8 %collective-permute-start.13 = (bf16[192,512]{1,0:T(8,128)(2,1)S(1)}, bf16[192,512]{1,0:T(8,128)(2,1)}, u32[]{:S(2)}, u32[]{:S(2)}) collective-permute-start(bf16[192,512]{1,0:T(8,128)(2,1)S(1)} %get-tuple-element.22), channel_id=1, source_target_pairs={{0,3},{1,0},{2,1},{3,2},{4,7},{5,4},{6,5},{7,6},{8,11},{9,8},{10,9... | collective-permute-start | bytes 589832 | tf_op jit(solution)/shard_map/ppermute | solution.py:391
  87.0 31.2 %collective-permute-start.16 = (bf16[2,2,1,96,384]{4,3,2,1,0:T(8,128)(2,1)S(1)}, bf16[2,2,1,96,384]{4,3,2,1,0:T(8,128)(2,1)S(1)}, u32[]{:S(2)}, u32[]{:S(2)}) collective-permute-start(bf16[2,2,1,96,384]{4,3,2,1,0:T(8,128)(2,1)S(1)} %dynamic-slice_convert_fusion.1), channel_id=1, source_target_pairs={{0,4},{4,0},{8,12},{12,8},{16,20},{20,16},{24,28},{28,24},{1,5},{5... | collective-permute-start | bytes 884744 | tf_op jit(solution)/shard_map/ppermute | solution.py:300
  104.8 7.5 %collective-permute-start.14 = (bf16[192,192]{1,0:T(8,128)(2,1)}, bf16[192,192]{1,0:T(8,128)(2,1)}, u32[]{:S(2)}, u32[]{:S(2)}) collective-permute-start(bf16[192,192]{1,0:T(8,128)(2,1)} %get-tuple-element.12), channel_id=1, source_target_pairs={{0,4},{4,8},{8,12},{12,16},{16,20},{20,24},{24,28},{1,5},{5,9},{9,... | collective-permute-start | bytes 221192 | tf_op jit(solution)/shard_map/ppermute | solution.py:411
  108.3 7.9 %collective-permute-start.15 = (bf16[192,192]{1,0:T(8,128)(2,1)}, bf16[192,192]{1,0:T(8,128)(2,1)}, u32[]{:S(2)}, u32[]{:S(2)}) collective-permute-start(bf16[192,192]{1,0:T(8,128)(2,1)} %get-tuple-element.13), channel_id=1, source_target_pairs={{4,0},{8,4},{12,8},{16,12},{20,16},{24,20},{28,24},{5,1},{9,5},{13... | collective-permute-start | bytes 221192 | tf_op jit(solution)/shard_map/ppermute | solution.py:410
  109.6 10.4 %collective-permute-start.19 = (bf16[2,2,1,96,384]{4,3,2,1,0:T(8,128)(2,1)S(1)}, bf16[2,2,1,96,384]{4,3,2,1,0:T(8,128)(2,1)S(1)}, u32[]{:S(2)}, u32[]{:S(2)}) collective-permute-start(bf16[2,2,1,96,384]{4,3,2,1,0:T(8,128)(2,1)S(1)} %dynamic-slice_convert_fusion), channel_id=1, source_target_pairs={{0,4},{4,0},{8,12},{12,8},{16,20},{20,16},{24,28},{28,24},{1,5},{5... | collective-permute-start | bytes 884744 | tf_op jit(solution)/shard_map/ppermute | solution.py:300
  118.3 6.2 %collective-permute-start.17 = (bf16[2,1,1,96,384]{4,3,2,1,0:T(8,128)(2,1)S(1)}, bf16[2,1,1,96,384]{4,3,2,1,0:T(8,128)(2,1)S(1)}, u32[]{:S(2)}, u32[]{:S(2)}) collective-permute-start(bf16[2,1,1,96,384]{4,3,2,1,0:T(8,128)(2,1)S(1)} %dynamic-slice_convert_fusion.3), channel_id=1, source_target_pairs={{0,8},{4,12},{8,0},{12,4},{16,24},{20,28},{24,16},{28,20},{1,9},{5... | collective-permute-start | bytes 442376 | tf_op jit(solution)/shard_map/ppermute | solution.py:300
  120.1 6.4 %collective-permute-start.20 = (bf16[2,1,1,96,384]{4,3,2,1,0:T(8,128)(2,1)S(1)}, bf16[2,1,1,96,384]{4,3,2,1,0:T(8,128)(2,1)S(1)}, u32[]{:S(2)}, u32[]{:S(2)}) collective-permute-start(bf16[2,1,1,96,384]{4,3,2,1,0:T(8,128)(2,1)S(1)} %dynamic-slice_convert_fusion.2), channel_id=1, source_target_pairs={{0,8},{4,12},{8,0},{12,4},{16,24},{20,28},{24,16},{28,20},{1,9},{5... | collective-permute-start | bytes 442376 | tf_op jit(solution)/shard_map/ppermute | solution.py:300
  124.5 7.1 %collective-permute-start.18 = (bf16[1,1,1,96,384]{4,3,2,1,0:T(8,128)(2,1)S(1)}, bf16[1,1,1,96,384]{4,3,2,1,0:T(8,128)(2,1)S(1)}, u32[]{:S(2)}, u32[]{:S(2)}) collective-permute-start(bf16[1,1,1,96,384]{4,3,2,1,0:T(8,128)(2,1)S(1)} %dynamic-slice_convert_fusion.5), channel_id=1, source_target_pairs={{0,16},{4,20},{8,24},{12,28},{16,0},{20,4},{24,8},{28,12},{1,17},{... | collective-permute-start | bytes 221192 | tf_op jit(solution)/shard_map/ppermute | solution.py:300
  126.5 6.6 %collective-permute-start.21 = (bf16[1,1,1,96,384]{4,3,2,1,0:T(8,128)(2,1)S(1)}, bf16[1,1,1,96,384]{4,3,2,1,0:T(8,128)(2,1)S(1)}, u32[]{:S(2)}, u32[]{:S(2)}) collective-permute-start(bf16[1,1,1,96,384]{4,3,2,1,0:T(8,128)(2,1)S(1)} %dynamic-slice_convert_fusion.4), channel_id=1, source_target_pairs={{0,16},{4,20},{8,24},{12,28},{16,0},{20,4},{24,8},{28,12},{1,17},{... | collective-permute-start | bytes 221192 | tf_op jit(solution)/shard_map/ppermute | solution.py:300
  (4 other events, 22.7 us)
